TPU v7x, 256 devices: a whole 4x4x8 slice. The times are simulated.
256 devices in a mesh: dp: 16 (over z, core), tensor: 4 (over y), corpus: 4 (over x).
Axes of the slice: x: 4, y: 4, z: 8, core: 2. Of those that a mesh axis runs over, the one named last changes fastest.
Arguments:
- queries: bfloat16 [4096, 2048], P(('dp', 'tensor', 'corpus')), may hold values from -24 to 24
- passages: bfloat16 [65536, 2048], P(('dp', 'corpus'), 'tensor'), may hold values from -6 to 6
- pos_ids: int32 [4096], P(('dp', 'tensor', 'corpus')), may hold values from 0 to 65535, as said below
- neg_ids: int32 [4096, 32], P(('dp', 'tensor', 'corpus')), may hold values from 0 to 65535, as said below
Outputs:
- grad_query: float32 [4096, 2048], P(('dp', 'tensor', 'corpus'))
- losses: float32 [4096], P(('dp', 'tensor', 'corpus'))
- grad_pass: float32 [65536, 2048], P(('dp', 'corpus'), 'tensor')
Inputs may be any that keep to these rules, and one draw needn't show every extreme that they name: `pos_ids`: together with neg_ids: the ids named by the 16 queries of one device, positives and negatives together, fall at most 16 times into one block of 1024 passage rows (rows b * 1024 to (b + 1) * 1024 - 1), and exactly 16 times into one block that is the same for every device. Ids may repeat. `neg_ids`: counted together with pos_ids as stated there.
All inputs are finite; a program needn't handle non-finite values.
Results may differ from a plain program's by a relative error of at most 0.0035.
Values may be sent and summed in bfloat16 or wider, within the bound.
A program may use at most 128 MiB of HBM per device.

v0:
```python
import jax
import jax.numpy as jnp
from jax import lax
from jax.sharding import PartitionSpec as P


def lookup_rows(row_table, asked_ids):
    return jnp.take(row_table, asked_ids, axis=0, mode="fill", fill_value=0)


def body(queries, passages, pos_ids, neg_ids):
    per_device, feat_width = queries.shape
    block_rows, shard_width = passages.shape
    neg_count = neg_ids.shape[1]
    owners = lax.axis_size("dp") * lax.axis_size("corpus")
    slot_count = 2 * per_device * (neg_count + 1) // owners
    score_scale = feat_width ** (-0.5)
    wanted = jnp.concatenate([pos_ids[:, None], neg_ids], axis=1).reshape(-1)
    owner_of = wanted // block_rows
    local_row = wanted % block_rows
    matches = (owner_of[:, None] == jnp.arange(owners)[None, :]).astype(jnp.int32)
    earlier = jnp.cumsum(matches, axis=0) - matches
    slot_of = owner_of * slot_count + jnp.sum(earlier * matches, axis=1)
    send_ids = jnp.full((owners * slot_count,), block_rows, jnp.int32).at[slot_of].set(local_row)
    send_ids = send_ids.reshape(owners, slot_count)
    row_table = lax.all_gather(passages, "tensor", axis=1, tiled=True)
    asked_ids = lax.all_to_all(send_ids, ("dp", "corpus"), split_axis=0, concat_axis=0, tiled=True)
    found = lookup_rows(row_table, asked_ids)
    fetched = lax.all_to_all(found, ("dp", "corpus"), split_axis=0, concat_axis=0, tiled=True)
    gathered = fetched.reshape(owners * slot_count, feat_width)[slot_of]
    gathered = gathered.reshape(per_device, neg_count + 1, feat_width)
    pos_rows = gathered[:, 0, :]
    neg_rows = gathered[:, 1:, :]
    in_batch = lax.all_gather(pos_rows, "dp", axis=0, tiled=True)
    columns = in_batch.shape[0]
    in_scores = (
        lax.dot_general(
            queries, in_batch, (((1,), (1,)), ((), ())), preferred_element_type=jnp.float32
        )
        * score_scale
    )
    neg_scores = (
        jnp.einsum("md,mkd->mk", queries, neg_rows, preferred_element_type=jnp.float32)
        * score_scale
    )
    logits = jnp.concatenate([in_scores, neg_scores], axis=1)
    row_max = jnp.max(logits, axis=1, keepdims=True)
    exponent = jnp.exp(logits - row_max)
    denominator = jnp.sum(exponent, axis=1, keepdims=True)
    own_col = lax.axis_index("dp") * per_device + jnp.arange(per_device)
    target = (jnp.arange(columns + neg_count)[None, :] == own_col[:, None]).astype(jnp.float32)
    losses = jnp.log(denominator[:, 0]) + row_max[:, 0] - jnp.sum(target * logits, axis=1)
    weights = (exponent / denominator - target).astype(jnp.bfloat16)
    in_weights = weights[:, :columns]
    neg_weights = weights[:, columns:]
    grad_query = jnp.dot(in_weights, in_batch, preferred_element_type=jnp.float32)
    grad_query = grad_query + jnp.einsum(
        "mk,mkd->md", neg_weights, neg_rows, preferred_element_type=jnp.float32
    )
    grad_query = grad_query * score_scale
    in_terms = lax.dot_general(
        in_weights, queries, (((0,), (0,)), ((), ())), preferred_element_type=jnp.float32
    )
    pos_grad = lax.psum_scatter(in_terms, "dp", scatter_dimension=0, tiled=True) * score_scale
    neg_grad = (
        neg_weights.astype(jnp.float32)[:, :, None]
        * queries.astype(jnp.float32)[:, None, :]
        * score_scale
    )
    row_grads = jnp.concatenate([pos_grad[:, None, :], neg_grad], axis=1).astype(jnp.bfloat16)
    row_grads = row_grads.reshape(-1, feat_width)
    grad_slots = (
        jnp.zeros((owners * slot_count, feat_width), jnp.bfloat16).at[slot_of].set(row_grads)
    )
    grad_slots = grad_slots.reshape(owners, slot_count, feat_width)
    arrived = lax.all_to_all(grad_slots, ("dp", "corpus"), split_axis=0, concat_axis=0, tiled=True)
    accum_grad = jnp.zeros((block_rows, feat_width), jnp.float32)
    accum_grad = accum_grad.at[asked_ids.reshape(-1)].add(
        arrived.reshape(-1, feat_width).astype(jnp.float32), mode="drop"
    )
    grad_pass = lax.psum_scatter(accum_grad, "tensor", scatter_dimension=1, tiled=True)
    return (grad_query, losses, grad_pass)


def solution(mesh):
    in_specs = (
        P(("dp", "tensor", "corpus"), None),
        P(("dp", "corpus"), "tensor"),
        P(("dp", "tensor", "corpus")),
        P(("dp", "tensor", "corpus"), None),
    )
    out_specs = (
        P(("dp", "tensor", "corpus"), None),
        P(("dp", "tensor", "corpus")),
        P(("dp", "corpus"), "tensor"),
    )
    return jax.shard_map(body, mesh=mesh, in_specs=in_specs, out_specs=out_specs, check_vma=False)
```

profile of v0, /device:TPU:1, one launch (start us, length us, event | category | flops | bytes accessed | tf_op | source)
XLA Modules:
  0.0 520.4 jit_solution(17081883421997860384)
XLA Ops:
  7.2 0.7 all-gather.4.cloned.1.call-update
  7.9 0.7 copy.13
  8.6 0.8 pad_add_fusion
  9.4 0.1 reshape.217
  9.5 0.1 reshape.218
  9.7 1.5 reduce-window.6
  11.2 0.3 slice_reduce_fusion
  11.5 0.1 bitcast_bitcast_fusion
  11.7 4.1 scatter_custom_fusion
  15.8 0.1 all_to_all.16
  15.8 22.0 %all_to_all.25 = s32[64,1,16]{2,1,0:T(1,128)S(1)} all-to-all(s32[64,1,16]{2,1,0:T(1,128)S(1)} %bitcast.53), channel_id=1, replica_groups=mesh['dp'=16,'tensor'=4,'corpus'=4] {'dp','corpus'}, dimensions={0} | all-to-all | bytes 8192 | tf_op jit(solution)/shard_map/all_to_all | solution.py:27
  37.8 0.1 reshape.229
  37.9 26.3 %all-gather.4.cloned.1.call-done = bf16[1024,2048]{1,0:T(8,128)(2,1)} async-done(((bf16[1024,512]{1,0:T(8,128)(2,1)}), bf16[1024,2048]{1,0:T(8,128)(2,1)}) %all-gather.4.cloned.1.call-update) | async-done | bytes 4194320 | tf_op jit(solution)/shard_map/all_gather | solution.py:26
  64.2 11.6 %gather_fusion = bf16[1024,2048]{1,0:T(8,128)(2,1)} fusion(bf16[1024,2048]{1,0:T(8,128)(2,1)} %all-gather.4.cloned.1.call-done, s32[1024]{0:T(1024)S(1)} %broadcast_clamp_fusion), kind=kCustom, calls=%fused_computation | custom fusion | bytes 8392704 | tf_op jit(solution)/shard_map/jit(_take)/gather | solution.py:8
  75.8 4.5 broadcast_select_fusion
  80.3 11.0 %all-to-all-start.1 = ((bf16[64,16,2048]{2,1,0:T(8,128)(2,1)}), bf16[64,16,2048]{2,1,0:T(8,128)(2,1)}, u32[]{:S(2)}, u32[]{:S(2)}) async-start(bf16[64,16,2048]{2,1,0:T(8,128)(2,1)} %broadcast_select_fusion), calls=%async_computation.1 | async-start | bytes 8388608 | tf_op jit(solution)/shard_map/all_to_all | solution.py:29
  91.3 0.0 all-gather.6.cloned.1.call-start
  91.4 93.5 %all-to-all-done.1 = bf16[64,16,2048]{2,1,0:T(8,128)(2,1)} async-done(((bf16[64,16,2048]{2,1,0:T(8,128)(2,1)}), bf16[64,16,2048]{2,1,0:T(8,128)(2,1)}, u32[]{:S(2)}, u32[]{:S(2)}) %all-to-all-start.1) | async-done | bytes 4194336 | tf_op jit(solution)/shard_map/all_to_all | solution.py:29
  184.9 9.0 %gather_fusion.1 = bf16[528,2048]{1,0:T(8,128)(2,1)S(1)} fusion(bf16[1024,2048]{1,0:T(8,128)(2,1)} %bitcast.6, s32[1024]{0:T(1024)S(1)} %pad_clamp_fusion), kind=kCustom, calls=%fused_computation.1 | custom fusion | bytes 4327488 | tf_op jit(solution)/shard_map/gather | solution.py:30
  193.9 1.9 reshape.222
  195.8 1.1 slice.34
  196.9 0.7 copy.17
  197.6 0.2 reduce-scatter.3.cloned.1.call-start
  197.8 2.4 fusion.8
  200.2 0.1 fusion.26
  200.4 34.0 %all-gather.6.cloned.1.call-done = bf16[256,1,2048]{2,0,1:T(8,128)(2,1)} async-done(((bf16[16,1,2048]{2,0,1:T(8,128)(2,1)}), bf16[256,1,2048]{2,0,1:T(8,128)(2,1)}) %all-gather.6.cloned.1.call-update) | async-done | bytes 1048592 | tf_op jit(solution)/shard_map/all_gather | solution.py:34
  234.4 1.7 fusion.27
  236.1 0.2 select_reduce_fusion
  236.3 0.1 subtract_convert_fusion
  236.4 1.8 fusion.18
  238.2 1.8 multiply_convert_fusion
  240.1 53.7 %reduce-scatter.3.cloned.1.call-done = f32[16,2048]{1,0:T(8,128)} async-done(((f32[256,2048]{1,0:T(8,128)}), f32[16,2048]{1,0:T(8,128)}) %reduce-scatter.3.cloned.1.call-update) | async-done | bytes 131088 | tf_op jit(solution)/shard_map/reduce_scatter | solution.py:64
  293.8 0.9 fusion.15
  294.7 0.1 copy.18
  294.8 2.4 pad_maximum_fusion
  297.2 1.8 reshape.255
  299.0 10.4 %scatter_custom_fusion.1 = bf16[1024,2048]{1,0:T(8,128)(2,1)} fusion(s32[528]{0:T(1024)S(1)} %fusion.23, bf16[528,2048]{1,0:T(8,128)(2,1)} %reshape.255, bf16[]{:T(256)} %constant.66.clone.1), kind=kCustom, calls=%fused_computation.13 | custom fusion | bytes 4194816 | tf_op jit(solution)/shard_map/scatter | solution.py:73
  309.4 10.7 %all-to-all-start.2 = ((bf16[64,16,2048]{2,1,0:T(8,128)(2,1)}), bf16[64,16,2048]{2,1,0:T(8,128)(2,1)}, u32[]{:S(2)}, u32[]{:S(2)}) async-start(bf16[64,16,2048]{2,1,0:T(8,128)(2,1)} %bitcast.46), calls=%async_computation.3 | async-start | bytes 8388608 | tf_op jit(solution)/shard_map/all_to_all | solution.py:76
  320.1 0.3 reduce-scatter.5.cloned.1.call-start
  320.4 0.5 broadcast.199
  320.9 0.7 reduce.10
  321.6 0.1 reshape.223
  321.7 91.9 %all-to-all-done.2 = bf16[64,16,2048]{2,1,0:T(8,128)(2,1)} async-done(((bf16[64,16,2048]{2,1,0:T(8,128)(2,1)}), bf16[64,16,2048]{2,1,0:T(8,128)(2,1)}, u32[]{:S(2)}, u32[]{:S(2)}) %all-to-all-start.2) | async-done | bytes 4194336 | tf_op jit(solution)/shard_map/all_to_all | solution.py:76
  413.7 18.3 %scatter_custom_fusion.2 = f32[1024,2048]{1,0:T(8,128)} fusion(s32[1024]{0:T(1024)S(1)} %bitcast.56, bf16[1024,2048]{1,0:T(8,128)(2,1)} %bitcast.18, f32[]{:T(128)} %constant.69.clone.1), kind=kCustom, calls=%fused_computation.5 | custom fusion | flops 4194304 | bytes 12582916 | tf_op jit(solution)/shard_map/scatter-add | solution.py:78
  432.0 0.5 add_subtract_fusion
  432.6 2.4 fusion.6
  434.9 0.9 fusion.3
  435.8 78.0 %reduce-scatter.5.cloned.1.call-done = f32[1024,512]{1,0:T(8,128)} async-done(((f32[1024,2048]{1,0:T(8,128)}), f32[1024,512]{1,0:T(8,128)}) %reduce-scatter.5.cloned.1.call-update) | async-done | bytes 2097168 | tf_op jit(solution)/shard_map/reduce_scatter | solution.py:81
  (23 shorter events, 0.3 us)
Async XLA Ops:
  7.2 57.1 %all-gather.4.cloned.1.call-start = ((), (), s32[]{:S(2)}) async-start(), calls=%async_computation.5 | async-start | bytes 5242880 | tf_op jit(solution)/shard_map/all_gather | solution.py:26
  80.3 104.6 %all-to-all-start.1 = ((bf16[64,16,2048]{2,1,0:T(8,128)(2,1)}), bf16[64,16,2048]{2,1,0:T(8,128)(2,1)}, u32[]{:S(2)}, u32[]{:S(2)}) async-start(bf16[64,16,2048]{2,1,0:T(8,128)(2,1)} %broadcast_select_fusion), calls=%async_computation.1 | async-start | bytes 8388608 | tf_op jit(solution)/shard_map/all_to_all | solution.py:29
  91.3 143.0 %all-gather.6.cloned.1.call-start = ((), (), s32[]{:S(2)}) async-start(), calls=%async_computation.8 | async-start | bytes 1114112 | tf_op jit(solution)/shard_map/all_gather | solution.py:34
  193.9 3.9 copy-start.1
  197.6 96.2 %reduce-scatter.3.cloned.1.call-start = ((), (), s32[]{:S(2)}) async-start(), calls=%async_computation.6 | async-start | bytes 2228224 | tf_op jit(solution)/shard_map/reduce_scatter | solution.py:64
  309.4 104.3 %all-to-all-start.2 = ((bf16[64,16,2048]{2,1,0:T(8,128)(2,1)}), bf16[64,16,2048]{2,1,0:T(8,128)(2,1)}, u32[]{:S(2)}, u32[]{:S(2)}) async-start(bf16[64,16,2048]{2,1,0:T(8,128)(2,1)} %bitcast.46), calls=%async_computation.3 | async-start | bytes 8388608 | tf_op jit(solution)/shard_map/all_to_all | solution.py:76
  320.1 193.7 %reduce-scatter.5.cloned.1.call-start = ((), (), s32[]{:S(2)}) async-start(), calls=%async_computation.7 | async-start | bytes 10485760 | tf_op jit(solution)/shard_map/reduce_scatter | solution.py:81
  432.0 2.9 copy-start
Sparse Core Ops, SparseCore 0:
  9.8 54.3 all-gather.3
  197.7 36.6 all-gather.5
  238.3 55.4 reduce-scatter.2
  432.2 81.6 reduce-scatter.4
where the time goes:
time: 521 us; the launch traced here: 520 us
  waiting for transfers between devices  378 us (73%)
  local copies, waits for them, and re-layouts  42.5 us (8%)
  other arithmetic  32.2 us (6%)
  starting transfers between devices  22.3 us (4%)
  blocking collectives  22 us (4%)
  between operations  14 us (3%)
  matrix products  9.2 us (2%)
    all_to_all x1, waiting for transfers between devices, body(): lax.all_to_all(found, ('dp', 'corpus'), split_axis=0, concat_axis=0, tile...  93.5 us
    all_to_all x1, waiting for transfers between devices, body(): lax.all_to_all(grad_slots, ('dp', 'corpus'), split_axis=0, concat_axis=0,...  91.9 us
    reduce_scatter x1, waiting for transfers between devices, body(): lax.psum_scatter(accum_grad, 'tensor', scatter_dimension=1, tiled=True)  78 us
    reduce_scatter x1, waiting for transfers between devices, body(): lax.psum_scatter(in_terms, 'dp', scatter_dimension=0, tiled=True)  53.7 us
    all_gather x1, waiting for transfers between devices, body(): in_batch = lax.all_gather(pos_rows, 'dp', axis=0, tiled=True)  34 us
    all_gather x1, waiting for transfers between devices, body(): row_table = lax.all_gather(passages, 'tensor', axis=1, tiled=True)  26.3 us
    all_to_all x1, blocking collectives, body(): lax.all_to_all(send_ids, ('dp', 'corpus'), split_axis=0, concat_axis=0, t...  22 us
    scatter-add x1, other arithmetic, body(): accum_grad.at[asked_ids.reshape(-1)]  18.3 us
  transfers between devices with their start and end apart: 6, of which 6 were waited for; matrix products, arithmetic and copies ran while one was open for 3% of the time, Pallas kernels for 0%

commit v1 on v0

--- a/solution.py
+++ b/solution.py
@@ -2,6 +2,18 @@
 import jax.numpy as jnp
 from jax import lax
 from jax.sharding import PartitionSpec as P
+
+
+def _search_racks(axis_name, w_in):
+    copies = []
+    for _ in range(jax.lax.axis_size(axis_name)):
+        copies.append(w_in)
+    return jnp.concatenate(
+        jax.lax.all_to_all(
+            jnp.stack(copies, axis=0), axis_name=axis_name, split_axis=0, concat_axis=0
+        ),
+        axis=1,
+    )
 
 
 def lookup_rows(row_table, asked_ids):
@@ -23,7 +35,7 @@
     slot_of = owner_of * slot_count + jnp.sum(earlier * matches, axis=1)
     send_ids = jnp.full((owners * slot_count,), block_rows, jnp.int32).at[slot_of].set(local_row)
     send_ids = send_ids.reshape(owners, slot_count)
-    row_table = lax.all_gather(passages, "tensor", axis=1, tiled=True)
+    row_table = _search_racks("tensor", passages)
     asked_ids = lax.all_to_all(send_ids, ("dp", "corpus"), split_axis=0, concat_axis=0, tiled=True)
     found = lookup_rows(row_table, asked_ids)
     fetched = lax.all_to_all(found, ("dp", "corpus"), split_axis=0, concat_axis=0, tiled=True)

time: 521 us -> 550 us (1.056)
  waiting for transfers between devices: 378 us -> 398 us
  local copies, waits for them, and re-layouts: 42.5 us -> 50.8 us
    all_to_all x0 -> x1, waiting for transfers between devices: none -> 47.9 us  [_search_racks(): jax.lax.all_to_all(jnp.stack(copies, axis=0), axis_name=axis_name, split_...]
    all_gather x1 -> x0, waiting for transfers between devices: 26.3 us -> none  [body(): row_table = lax.all_gather(passages, 'tensor', axis=1, tiled=True)]
  transfers between devices with their start and end apart: 6 -> 6, of which waited for: 6 -> 6; matrix products, arithmetic and copies ran while one was open for 3% -> 2% of each run, Pallas kernels for 0% -> 0%
where the time goes in v1:
time: 550 us; the launch traced here: 549 us
  waiting for transfers between devices  398 us (72%)
  local copies, waits for them, and re-layouts  50.8 us (9%)
  other arithmetic  32.2 us (6%)
  starting transfers between devices  23 us (4%)
  blocking collectives  22 us (4%)
  between operations  14 us (3%)
  matrix products  9.2 us (2%)
    all_to_all x1, waiting for transfers between devices, body(): lax.all_to_all(found, ('dp', 'corpus'), split_axis=0, concat_axis=0, tile...  93.5 us
    all_to_all x1, waiting for transfers between devices, body(): lax.all_to_all(grad_slots, ('dp', 'corpus'), split_axis=0, concat_axis=0,...  91.9 us
    reduce_scatter x1, waiting for transfers between devices, body(): lax.psum_scatter(accum_grad, 'tensor', scatter_dimension=1, tiled=True)  78 us
    reduce_scatter x1, waiting for transfers between devices, body(): lax.psum_scatter(in_terms, 'dp', scatter_dimension=0, tiled=True)  53.7 us
    all_to_all x1, waiting for transfers between devices, _search_racks(): jax.lax.all_to_all(jnp.stack(copies, axis=0), axis_name=axis_name, split_...  47.9 us
    all_gather x1, waiting for transfers between devices, body(): in_batch = lax.all_gather(pos_rows, 'dp', axis=0, tiled=True)  33.2 us
    all_to_all x1, blocking collectives, body(): lax.all_to_all(send_ids, ('dp', 'corpus'), split_axis=0, concat_axis=0, t...  22 us
    scatter-add x1, other arithmetic, body(): accum_grad.at[asked_ids.reshape(-1)]  18.3 us
  transfers between devices with their start and end apart: 6, of which 6 were waited for; matrix products, arithmetic and copies ran while one was open for 2% of the time, Pallas kernels for 0%

profile of v1, /device:TPU:1, one launch (start us, length us, event | category | flops | bytes accessed | tf_op | source)
XLA Modules:
  0.0 549.5 jit_solution(5015490743933873131)
XLA Ops:
  7.2 0.7 copy.13
  7.9 0.8 pad_add_fusion
  8.7 0.1 reshape.225
  8.8 0.1 reshape.226
  8.9 1.5 reduce-window.6
  10.4 0.3 slice_reduce_fusion
  10.7 0.1 bitcast_bitcast_fusion
  10.9 4.1 scatter_custom_fusion
  15.1 22.0 %all_to_all.30 = s32[64,1,16]{2,1,0:T(1,128)S(1)} all-to-all(s32[64,1,16]{2,1,0:T(1,128)S(1)} %bitcast.57), channel_id=1, replica_groups=mesh['dp'=16,'tensor'=4,'corpus'=4] {'dp','corpus'}, dimensions={0} | all-to-all | bytes 8192 | tf_op jit(solution)/shard_map/all_to_all | solution.py:39
  37.1 3.5 stack.2
  40.6 4.9 all-to-all-start.1
  45.5 0.1 reshape.239
  45.6 47.9 %all-to-all-done.1 = bf16[4,1024,512]{2,1,0:T(8,128)(2,1)} async-done(((bf16[4,1024,512]{2,1,0:T(8,128)(2,1)}), bf16[4,1024,512]{2,1,0:T(8,128)(2,1)}, u32[]{:S(2)}, u32[]{:S(2)}) %all-to-all-start.1) | async-done | bytes 4194336 | tf_op jit(solution)/shard_map/all_to_all | solution.py:12
  93.5 4.8 copy.26
  98.3 11.6 %gather_fusion = bf16[1024,2048]{1,0:T(8,128)(2,1)} fusion(bf16[1024,2048]{1,0:T(8,128)(2,1)} %bitcast.49, s32[1024]{0:T(1024)S(1)} %broadcast_clamp_fusion), kind=kCustom, calls=%fused_computation | custom fusion | bytes 8392704 | tf_op jit(solution)/shard_map/jit(_take)/gather | solution.py:20
  109.8 4.5 broadcast_select_fusion
  114.3 6.8 %all-to-all-start.2 = ((bf16[64,16,2048]{2,1,0:T(8,128)(2,1)}), bf16[64,16,2048]{2,1,0:T(8,128)(2,1)}, u32[]{:S(2)}, u32[]{:S(2)}) async-start(bf16[64,16,2048]{2,1,0:T(8,128)(2,1)} %broadcast_select_fusion), calls=%async_computation.2 | async-start | bytes 8388608 | tf_op jit(solution)/shard_map/all_to_all | solution.py:41
  121.3 93.5 %all-to-all-done.2 = bf16[64,16,2048]{2,1,0:T(8,128)(2,1)} async-done(((bf16[64,16,2048]{2,1,0:T(8,128)(2,1)}), bf16[64,16,2048]{2,1,0:T(8,128)(2,1)}, u32[]{:S(2)}, u32[]{:S(2)}) %all-to-all-start.2) | async-done | bytes 4194336 | tf_op jit(solution)/shard_map/all_to_all | solution.py:41
  214.8 9.0 %gather_fusion.1 = bf16[528,2048]{1,0:T(8,128)(2,1)S(1)} fusion(bf16[1024,2048]{1,0:T(8,128)(2,1)} %bitcast.7, s32[1024]{0:T(1024)S(1)} %pad_clamp_fusion), kind=kCustom, calls=%fused_computation.1 | custom fusion | bytes 4327488 | tf_op jit(solution)/shard_map/gather | solution.py:42
  223.8 1.9 reshape.232
  225.7 1.1 slice.34
  226.8 0.7 copy.18
  227.5 0.2 reduce-scatter.3.cloned.1.call-start
  227.8 2.4 fusion.8
  230.2 0.1 fusion.26
  230.3 33.2 %all-gather.3.cloned.1.call-done = bf16[256,1,2048]{2,0,1:T(8,128)(2,1)} async-done(((bf16[16,1,2048]{2,0,1:T(8,128)(2,1)}), bf16[256,1,2048]{2,0,1:T(8,128)(2,1)}) %all-gather.3.cloned.1.call-update) | async-done | bytes 1048592 | tf_op jit(solution)/shard_map/all_gather | solution.py:46
  263.4 1.7 fusion.27
  265.2 0.2 select_reduce_fusion
  265.4 0.1 subtract_convert_fusion
  265.5 1.8 fusion.18
  267.3 1.8 multiply_convert_fusion
  269.1 53.7 %reduce-scatter.3.cloned.1.call-done = f32[16,2048]{1,0:T(8,128)} async-done(((f32[256,2048]{1,0:T(8,128)}), f32[16,2048]{1,0:T(8,128)}) %reduce-scatter.3.cloned.1.call-update) | async-done | bytes 131088 | tf_op jit(solution)/shard_map/reduce_scatter | solution.py:76
  322.8 0.9 fusion.15
  323.8 0.1 copy.19
  323.9 2.4 pad_maximum_fusion
  326.3 1.8 reshape.265
  328.0 10.4 %scatter_custom_fusion.1 = bf16[1024,2048]{1,0:T(8,128)(2,1)} fusion(s32[528]{0:T(1024)S(1)} %fusion.23, bf16[528,2048]{1,0:T(8,128)(2,1)} %reshape.265, bf16[]{:T(256)} %constant.66.clone.1), kind=kCustom, calls=%fused_computation.13 | custom fusion | bytes 4194816 | tf_op jit(solution)/shard_map/scatter | solution.py:85
  338.4 10.8 %all-to-all-start.3 = ((bf16[64,16,2048]{2,1,0:T(8,128)(2,1)}), bf16[64,16,2048]{2,1,0:T(8,128)(2,1)}, u32[]{:S(2)}, u32[]{:S(2)}) async-start(bf16[64,16,2048]{2,1,0:T(8,128)(2,1)} %bitcast.50), calls=%async_computation.4 | async-start | bytes 8388608 | tf_op jit(solution)/shard_map/all_to_all | solution.py:88
  349.2 0.3 reduce-scatter.5.cloned.1.call-start
  349.5 0.5 broadcast.201
  350.0 0.7 reduce.10
  350.7 0.1 reshape.233
  350.8 91.9 %all-to-all-done.3 = bf16[64,16,2048]{2,1,0:T(8,128)(2,1)} async-done(((bf16[64,16,2048]{2,1,0:T(8,128)(2,1)}), bf16[64,16,2048]{2,1,0:T(8,128)(2,1)}, u32[]{:S(2)}, u32[]{:S(2)}) %all-to-all-start.3) | async-done | bytes 4194336 | tf_op jit(solution)/shard_map/all_to_all | solution.py:88
  442.7 18.3 %scatter_custom_fusion.2 = f32[1024,2048]{1,0:T(8,128)} fusion(s32[1024]{0:T(1024)S(1)} %bitcast.60, bf16[1024,2048]{1,0:T(8,128)(2,1)} %bitcast.19, f32[]{:T(128)} %constant.69.clone.1), kind=kCustom, calls=%fused_computation.5 | custom fusion | flops 4194304 | bytes 12582916 | tf_op jit(solution)/shard_map/scatter-add | solution.py:90
  461.1 0.5 add_subtract_fusion
  461.6 2.4 fusion.6
  464.0 0.9 fusion.3
  464.9 78.0 %reduce-scatter.5.cloned.1.call-done = f32[1024,512]{1,0:T(8,128)} async-done(((f32[1024,2048]{1,0:T(8,128)}), f32[1024,512]{1,0:T(8,128)}) %reduce-scatter.5.cloned.1.call-update) | async-done | bytes 2097168 | tf_op jit(solution)/shard_map/reduce_scatter | solution.py:93
  (24 shorter events, 0.4 us)
Async XLA Ops:
  40.6 52.9 %all-to-all-start.1 = ((bf16[4,1024,512]{2,1,0:T(8,128)(2,1)}), bf16[4,1024,512]{2,1,0:T(8,128)(2,1)}, u32[]{:S(2)}, u32[]{:S(2)}) async-start(bf16[4,1024,512]{2,1,0:T(8,128)(2,1)} %stack.2), calls=%async_computation.1 | async-start | bytes 8388608 | tf_op jit(solution)/shard_map/all_to_all | solution.py:12
  114.3 100.4 %all-to-all-start.2 = ((bf16[64,16,2048]{2,1,0:T(8,128)(2,1)}), bf16[64,16,2048]{2,1,0:T(8,128)(2,1)}, u32[]{:S(2)}, u32[]{:S(2)}) async-start(bf16[64,16,2048]{2,1,0:T(8,128)(2,1)} %broadcast_select_fusion), calls=%async_computation.2 | async-start | bytes 8388608 | tf_op jit(solution)/shard_map/all_to_all | solution.py:41
  121.2 142.2 %all-gather.3.cloned.1.call-start = ((), (), s32[]{:S(2)}) async-start(), calls=%async_computation.8 | async-start | bytes 1114112 | tf_op jit(solution)/shard_map/all_gather | solution.py:46
  223.8 3.9 copy-start.1
  227.5 95.3 %reduce-scatter.3.cloned.1.call-start = ((), (), s32[]{:S(2)}) async-start(), calls=%async_computation.6 | async-start | bytes 2228224 | tf_op jit(solution)/shard_map/reduce_scatter | solution.py:76
  338.4 104.3 %all-to-all-start.3 = ((bf16[64,16,2048]{2,1,0:T(8,128)(2,1)}), bf16[64,16,2048]{2,1,0:T(8,128)(2,1)}, u32[]{:S(2)}, u32[]{:S(2)}) async-start(bf16[64,16,2048]{2,1,0:T(8,128)(2,1)} %bitcast.50), calls=%async_computation.4 | async-start | bytes 8388608 | tf_op jit(solution)/shard_map/all_to_all | solution.py:88
  349.2 193.7 %reduce-scatter.5.cloned.1.call-start = ((), (), s32[]{:S(2)}) async-start(), calls=%async_computation.7 | async-start | bytes 10485760 | tf_op jit(solution)/shard_map/reduce_scatter | solution.py:93
  461.1 2.9 copy-start
Sparse Core Ops, SparseCore 0:
  227.6 35.7 all-gather.2
  267.4 55.3 reduce-scatter.2
  461.2 81.6 reduce-scatter.4
